TPU v7x, 128 devices: a whole 4x4x4 slice. The times are simulated.
128 devices in a mesh: row: 16 (over z_hi, x, core), col: 8 (over y, z_lo).
Axes of the slice: x: 4, y: 4, z: 4 (z_hi: 2, z_lo: 2; z = z_hi * 2 + z_lo), core: 2. Of those that a mesh axis runs over, the one named last changes fastest.
Arguments:
- before_scan: float32 [4, 4096, 8192], P(None, 'row', 'col'), may hold values from -40 to 40
- after_scan: float32 [4, 4096, 8192], P(None, 'row', 'col'), may hold values from -40 to 40
- drift_offsets: int32 [2, 4, 16, 8], P(None, None, 'row', 'col'), may hold values from -128 to 128, as said below
- drift_fractions: int32 [2, 4, 16, 8], P(None, None, 'row', 'col'), may hold values from 0 to 255
Outputs:
- band_field: float32 [4, 4096, 8192], P(None, 'row', 'col')
- slope_field: float32 [4, 4096, 8192], P(None, 'row', 'col')
- surface_params: float32 [2, 4], replicated
Inputs may be any that keep to these rules, and one draw needn't show every extreme that they name: `drift_offsets`: for every scan and tile, the cells a tile reads (its own cells shifted by its offsets, widened by one row and column before and two after) lie inside the window. In every scan the first tile has offsets 128, 128 and the last tile minus 128, minus 128.
All inputs are finite; a program needn't handle non-finite values.
Results may differ from a plain program's by a relative error of at most 0.00014.
Values sent between devices are 32-bit elements; how exact they have to be, the bound alone decides.
No kernel may reach another device: no remote copies, remote signals or barrier semaphores. Data moves between devices by JAX's collectives and lax.ppermute only.
A program may use at most 128 MiB of HBM per device.

v0:
```python
import math
import jax
import jax.numpy as jnp
from jax import lax
from jax.sharding import PartitionSpec as P

LS = 5
SR = 4
LCUT = 1600
BLOCK = 16
DRIFT = 128
ALPHA = math.sqrt(math.log(2.0) / math.pi)
SPACING = 0.5
EPSILON = 1e-06
HIGHEST = lax.Precision.HIGHEST


def with_halo(value, sides, width):
    for axis, dim in sides:
        count, length = (lax.axis_size(axis), value.shape[dim])
        up = [(i, (i + 1) % count) for i in range(count - 1)]
        down = [(j, i) for i, j in up]
        last = lax.slice_in_dim(value, length - width, length, axis=dim)
        leading = lax.slice_in_dim(value, 0, width, axis=dim)
        before = lax.ppermute(last, axis, up)
        after = lax.ppermute(leading, axis, down)
        value = jnp.concatenate([before, value, after], axis=dim)
    return value


def cubic_weights(fraction):
    position = fraction.astype(jnp.float32) / 256.0
    square = position * position
    cube_term = square * position
    return (
        0.5 * (2.0 * square - cube_term - position),
        0.5 * (3.0 * cube_term - 5.0 * square + 2.0),
        0.5 * (4.0 * square - 3.0 * cube_term + position),
        0.5 * (cube_term - square),
    )


def interpolate(window, row_taps, col_taps):
    height = window.shape[0] - 3
    length = window.shape[1] - 3
    across = (
        row_taps[0] * window[0:height]
        + row_taps[1] * window[1 : height + 1]
        + row_taps[2] * window[2 : height + 2]
        + row_taps[3] * window[3 : height + 3]
    )
    return (
        col_taps[0] * across[:, 0:length]
        + col_taps[1] * across[:, 1 : length + 1]
        + col_taps[2] * across[:, 2 : length + 2]
        + col_taps[3] * across[:, 3 : length + 3]
    )


def resample(after_scan, drift_offsets, drift_fractions):
    height, length = (after_scan.shape[1], after_scan.shape[2])
    margin = DRIFT + 2
    widened = with_halo(after_scan, (("row", 1), ("col", 2)), margin)
    row_taps = jnp.stack(cubic_weights(drift_fractions[0, :, 0, 0]), axis=-1)
    col_taps = jnp.stack(cubic_weights(drift_fractions[1, :, 0, 0]), axis=-1)

    def one_scan(window, row_shift, col_shift, row_weights, col_weights):
        source = lax.dynamic_slice(
            window, (margin - 1 + row_shift, margin - 1 + col_shift), (height + 3, length + 3)
        )
        return interpolate(source, row_weights, col_weights)

    return jax.vmap(one_scan)(
        widened, drift_offsets[0, :, 0, 0], drift_offsets[1, :, 0, 0], row_taps, col_taps
    )


def short_taps():
    return [math.exp(-math.pi * (offset / (ALPHA * LS)) ** 2) for offset in range(-SR, SR + 1)]


def short_filter(widened, height, length):
    kernel_taps = short_taps()
    column_index = (
        lax.axis_index("col") * length - SR + jnp.arange(length + 2 * SR, dtype=jnp.int32)
    )
    column_inside = ((column_index >= 0) & (column_index < length * lax.axis_size("col"))).astype(
        jnp.float32
    )
    summed = kernel_taps[0] * widened[:, :, 0:length]
    weight = kernel_taps[0] * column_inside[0:length]
    for offset in range(1, 2 * SR + 1):
        summed = summed + kernel_taps[offset] * widened[:, :, offset : offset + length]
        weight = weight + kernel_taps[offset] * column_inside[offset : offset + length]
    across = summed / weight
    row_index = lax.axis_index("row") * height - SR + jnp.arange(height + 2 * SR, dtype=jnp.int32)
    row_inside = ((row_index >= 0) & (row_index < height * lax.axis_size("row"))).astype(
        jnp.float32
    )
    summed = kernel_taps[0] * across[:, 0:height, :]
    weight = kernel_taps[0] * row_inside[0:height]
    for offset in range(1, 2 * SR + 1):
        summed = summed + kernel_taps[offset] * across[:, offset : offset + height, :]
        weight = weight + kernel_taps[offset] * row_inside[offset : offset + height]
    return summed / weight[:, None]


def coarse_means(surface):
    scans, height, length = surface.shape
    return surface.reshape(scans, height // BLOCK, BLOCK, length // BLOCK, BLOCK).mean(axis=(2, 4))


def gauss_block(source, target):
    distance = ((source[:, None] - target[None, :]) * BLOCK).astype(jnp.float32) / (ALPHA * LCUT)
    return jnp.exp(-math.pi * distance * distance)


def long_cols(coarse):
    width = coarse.shape[2]
    target = lax.axis_index("col") * width + jnp.arange(width, dtype=jnp.int32)
    portion = lax.all_gather(coarse, "col", axis=2, tiled=True)
    source = jnp.arange(portion.shape[2], dtype=jnp.int32)
    matrix = gauss_block(source, target)
    summed = jnp.einsum("frk,kc->frc", portion, matrix, precision=HIGHEST)
    weight = jnp.sum(matrix, axis=0)
    return summed / weight


def long_rows(surface):
    rows_here = surface.shape[1]
    target = lax.axis_index("row") * rows_here + jnp.arange(rows_here, dtype=jnp.int32)
    portion = lax.all_gather(surface, "row", axis=1, tiled=True)
    source = jnp.arange(portion.shape[1], dtype=jnp.int32)
    matrix = gauss_block(target, source)
    summed = jnp.einsum("rk,fkc->frc", matrix, portion, precision=HIGHEST)
    weight = jnp.sum(matrix, axis=1)
    return summed / weight[:, None]


def upsample_matrix(fine_index, coarse_index, coarse_count):
    numerator = 2 * fine_index + 1 - BLOCK
    lower_index = numerator // (2 * BLOCK)
    fraction = (numerator - lower_index * (2 * BLOCK)).astype(jnp.float32) / (2.0 * BLOCK)
    outside = (lower_index < 0) | (lower_index >= coarse_count - 1)
    fraction = jnp.where(outside, jnp.zeros_like(fraction), fraction)
    lower_index = jnp.clip(lower_index, 0, coarse_count - 1)
    first_part = (coarse_index[None, :] == lower_index[:, None]).astype(jnp.float32) * (
        1.0 - fraction
    )[:, None]
    second_part = (coarse_index[None, :] == (lower_index + 1)[:, None]).astype(
        jnp.float32
    ) * fraction[:, None]
    return first_part + second_part


def upsample(wavy_coarse, height, length):
    coarse_rows, coarse_cols = (wavy_coarse.shape[1], wavy_coarse.shape[2])
    widened_coarse = with_halo(wavy_coarse, (("row", 1), ("col", 2)), 1)
    row_fine = lax.axis_index("row") * height + jnp.arange(height, dtype=jnp.int32)
    row_blocks = (
        lax.axis_index("row") * coarse_rows - 1 + jnp.arange(coarse_rows + 2, dtype=jnp.int32)
    )
    col_fine = lax.axis_index("col") * length + jnp.arange(length, dtype=jnp.int32)
    col_blocks = (
        lax.axis_index("col") * coarse_cols - 1 + jnp.arange(coarse_cols + 2, dtype=jnp.int32)
    )
    row_up = upsample_matrix(row_fine, row_blocks, coarse_rows * lax.axis_size("row"))
    col_up = upsample_matrix(col_fine, col_blocks, coarse_cols * lax.axis_size("col"))
    row_mixed = jnp.einsum("pa,sab->spb", row_up, widened_coarse, precision=HIGHEST)
    return jnp.einsum("spb,qb->spq", row_mixed, col_up, precision=HIGHEST)


def slopes(surface):
    height, length = (surface.shape[1], surface.shape[2])
    bordered = with_halo(surface, (("row", 1), ("col", 2)), 1)
    column_index = lax.axis_index("col") * length + jnp.arange(length, dtype=jnp.int32)
    row_index = lax.axis_index("row") * height + jnp.arange(height, dtype=jnp.int32)
    column_mask = (
        (column_index >= 1) & (column_index <= length * lax.axis_size("col") - 2)
    ).astype(jnp.float32)
    row_mask = ((row_index >= 1) & (row_index <= height * lax.axis_size("row") - 2)).astype(
        jnp.float32
    )
    along_cols = (bordered[:, 1:-1, 2:] - bordered[:, 1:-1, :-2]) / (2.0 * SPACING) * column_mask
    along_rows = (
        (bordered[:, 2:, 1:-1] - bordered[:, :-2, 1:-1]) / (2.0 * SPACING) * row_mask[:, None]
    )
    return along_cols * along_cols + along_rows * along_rows


def body(before_scan, after_scan, drift_offsets, drift_fractions):
    height, length = (before_scan.shape[1], before_scan.shape[2])
    shifted = resample(after_scan, drift_offsets, drift_fractions)
    difference = before_scan - shifted
    widened = with_halo(difference, (("row", 1), ("col", 2)), SR)
    smooth = short_filter(widened, height, length)
    coarse = coarse_means(smooth)
    wavy_coarse = long_rows(long_cols(coarse))
    waviness = upsample(wavy_coarse, height, length)
    band_field = smooth - waviness
    slope_field = slopes(band_field)
    height_sq = jnp.sum(band_field * band_field, axis=(1, 2))
    slope_sum = jnp.sum(slope_field, axis=(1, 2))
    height_all, slope_all = lax.psum((height_sq, slope_sum), ("row", "col"))
    total_cells = height * lax.axis_size("row") * length * lax.axis_size("col")
    surface_params = jnp.sqrt(jnp.stack([height_all, slope_all]) / total_cells + EPSILON)
    return (band_field, slope_field, surface_params)


def solution(mesh):
    in_specs = (
        P(None, "row", "col"),
        P(None, "row", "col"),
        P(None, None, "row", "col"),
        P(None, None, "row", "col"),
    )
    out_specs = (P(None, "row", "col"), P(None, "row", "col"), P())
    return jax.shard_map(body, mesh=mesh, in_specs=in_specs, out_specs=out_specs, check_vma=False)
```

profile of v0, /device:TPU:1, one launch (start us, length us, event | category | flops | bytes accessed | tf_op | source)
XLA Modules:
  0.0 455.7 jit_solution(10664465496469987918)
XLA Ops:
  0.6 3.2 fusion.118
  3.9 1.4 copy.42
  5.3 4.5 collective-permute-start
  9.8 2.7 copy.43
  12.5 2.0 collective-permute-start.1
  14.5 5.2 %copy.28 = f32[4,256,1024]{1,0,2:T(4,128)} copy(f32[4,256,1024]{2,1,0:T(8,128)} %param.5) | data formatting | bytes 8388608 | tf_op args[1]
  19.9 13.1 %collective-permute-done = f32[4,130,1024]{2,0,1:T(4,128)} collective-permute-done((f32[4,130,1024]{2,0,1:T(4,128)S(1)}, f32[4,130,1024]{2,0,1:T(4,128)}, u32[]{:S(2)}, u32[]{:S(2)}) %collective-permute-start) | collective-permute-done | bytes 2129952 | tf_op jit(solution)/shard_map/ppermute | solution.py:25
  33.1 6.2 %copy.27 = f32[4,130,1024]{1,0,2:T(4,128)} copy(f32[4,130,1024]{2,0,1:T(4,128)} %collective-permute-done) | data formatting | bytes 4259840 | tf_op jit(solution)/shard_map/ppermute | solution.py:25
  39.3 1.3 collective-permute-done.1
  40.6 6.2 %copy.29 = f32[4,130,1024]{1,0,2:T(4,128)} copy(f32[4,130,1024]{2,0,1:T(4,128)} %collective-permute-done.1) | data formatting | bytes 4259840 | tf_op jit(solution)/shard_map/ppermute | solution.py:26
  46.8 3.5 pad_maximum_fusion.13
  50.3 3.8 collective-permute-start.2
  54.1 1.5 collective-permute-start.3
  56.2 40.7 %collective-permute-done.2 = f32[4,516,130]{1,0,2:T(4,128)S(1)} collective-permute-done((f32[4,516,130]{1,0,2:T(4,128)S(1)}, f32[4,516,130]{1,0,2:T(4,128)S(1)}, u32[]{:S(2)}, u32[]{:S(2)}) %collective-permute-start.2) | collective-permute-done | bytes 1073312 | tf_op jit(solution)/shard_map/ppermute | solution.py:25
  97.0 29.5 %pad_maximum_fusion = f32[4,516,1284]{1,0,2:T(4,128)} fusion(f32[4,516,130]{1,0,2:T(4,128)S(1)} %collective-permute-done.3, f32[4,130,1024]{1,0,2:T(4,128)} %copy.29, f32[4,256,1024]{1,0,2:T(4,128)S(1)} %copy-done.2, f32[4,130,1024]{1,0,2:T(4,128)} %copy.27, f32[4,516,130]{1,0,2:T(4,128)S(1)} %collective-permute-done.2), kind=kLoop, calls=%fused_computation.2 | loop fusion | flops 10600704 | bytes 21201408 | tf_op jit(solution)/shard_map/concatenate | solution.py:27
  126.4 15.3 %copy.30 = f32[4,516,1284]{2,1,0:T(8,128)} copy(f32[4,516,1284]{1,0,2:T(4,128)} %pad_maximum_fusion) | data formatting | bytes 21201408
  141.7 21.6 %while.1 = (s32[]{:T(128)}, f32[4,516,1284]{2,1,0:T(8,128)}, s32[4,3]{1,0:T(4,128)S(1)}, f32[4,259,1027]{2,1,0:T(8,128)}, s32[]{:T(128)}) while((s32[]{:T(128)}, f32[4,516,1284]{2,1,0:T(8,128)}, s32[4,3]{1,0:T(4,128)S(1)}, f32[4,259,1027]{2,1,0:T(8,128)}, s32[]{:T(128)}) %tuple.51), condition=%wide.while_cond, body=%wide.while_body.sunk | while | flops 2 | bytes 2435185 | solution.py:68
  141.7 0.7 fusion.124
  142.3 4.8 %dynamic-slice_dynamic-update-slice_fusion.2 = f32[4,259,1027]{2,1,0:T(8,128)} fusion(f32[4,259,1027]{2,1,0:T(8,128)} %get-tuple-element.118, s32[]{:T(128)} %get-tuple-element.115, f32[4,516,1284]{2,1,0:T(8,128)} %get-tuple-element.121, s32[]{:T(128)} %bitcast.84, s32[]{:T(128)} %bitcast.85, s32[]{:T(128)} %bitcast.86), kind=kLoop, calls=%fused_computation.clone.1 | loop fusion | bytes 2435072 | tf_op jit(solution)/shard_map/vmap()/gather
  147.1 0.7 fusion.124
  147.8 4.7 %dynamic-slice_dynamic-update-slice_fusion.2 = f32[4,259,1027]{2,1,0:T(8,128)} fusion(f32[4,259,1027]{2,1,0:T(8,128)} %get-tuple-element.118, s32[]{:T(128)} %get-tuple-element.115, f32[4,516,1284]{2,1,0:T(8,128)} %get-tuple-element.121, s32[]{:T(128)} %bitcast.84, s32[]{:T(128)} %bitcast.85, s32[]{:T(128)} %bitcast.86), kind=kLoop, calls=%fused_computation.clone.1 | loop fusion | bytes 2435072 | tf_op jit(solution)/shard_map/vmap()/gather
  152.5 0.7 fusion.124
  153.1 4.7 %dynamic-slice_dynamic-update-slice_fusion.2 = f32[4,259,1027]{2,1,0:T(8,128)} fusion(f32[4,259,1027]{2,1,0:T(8,128)} %get-tuple-element.118, s32[]{:T(128)} %get-tuple-element.115, f32[4,516,1284]{2,1,0:T(8,128)} %get-tuple-element.121, s32[]{:T(128)} %bitcast.84, s32[]{:T(128)} %bitcast.85, s32[]{:T(128)} %bitcast.86), kind=kLoop, calls=%fused_computation.clone.1 | loop fusion | bytes 2435072 | tf_op jit(solution)/shard_map/vmap()/gather
  157.8 0.7 fusion.124
  158.5 4.7 %dynamic-slice_dynamic-update-slice_fusion.2 = f32[4,259,1027]{2,1,0:T(8,128)} fusion(f32[4,259,1027]{2,1,0:T(8,128)} %get-tuple-element.118, s32[]{:T(128)} %get-tuple-element.115, f32[4,516,1284]{2,1,0:T(8,128)} %get-tuple-element.121, s32[]{:T(128)} %bitcast.84, s32[]{:T(128)} %bitcast.85, s32[]{:T(128)} %bitcast.86), kind=kLoop, calls=%fused_computation.clone.1 | loop fusion | bytes 2435072 | tf_op jit(solution)/shard_map/vmap()/gather
  163.2 9.2 %multiply_add_fusion = f32[4,256,1027]{2,1,0:T(8,128)S(1)} fusion(f32[4,259,1027]{2,1,0:T(8,128)} %get-tuple-element.10, f32[4]{0:T(128)S(1)} %get-tuple-element.67, f32[4]{0:T(128)S(1)} %get-tuple-element.62, f32[4]{0:T(128)S(1)} %get-tuple-element.64, f32[4]{0:T(128)S(1)} %get-tuple-element.63), kind=kLoop, calls=%fused_computation.5 | loop fusion | flops 7361536 | bytes 21033024 | tf_op jit(solution)/shard_map/vmap()/add | solution.py:47
  172.5 3.4 fusion.25
  176.0 17.8 %collective-permute-start.4 = (f32[4,4,1024]{2,1,0:T(4,128)S(1)}, f32[4,4,1024]{2,1,0:T(4,128)S(1)}, u32[]{:S(2)}, u32[]{:S(2)}) collective-permute-start(f32[4,4,1024]{2,1,0:T(4,128)S(1)} %get-tuple-element.53), channel_id=1, source_target_pairs={{0,8},{8,16},{16,24},{24,32},{32,40},{40,48},{48,56},{56,64},{64,7... | collective-permute-start | bytes 196616 | tf_op jit(solution)/shard_map/ppermute | solution.py:25
  193.8 1.9 collective-permute-start.5
  195.8 3.6 collective-permute-done.5
  199.4 0.6 pad_maximum_fusion.2
  200.2 0.3 copy.32
  200.4 4.1 collective-permute-start.6
  204.6 0.3 copy.34
  204.8 1.5 collective-permute-start.7
  206.6 3.0 collective-permute-done.7
  209.9 7.4 %maximum_maximum_fusion = (f32[4,264,1028]{2,1,0:T(8,128)S(1)}, f32[4,264,1028]{2,1,0:T(8,128)}) fusion(f32[4,4,1024]{2,1,0:T(4,128)S(1)} %collective-permute-done.5, f32[4,256,1024]{2,1,0:T(8,128)} %copy-done, f32[4,4,1024]{2,1,0:T(4,128)S(1)} %collective-permute-done.4, f32[4,264,4]{2,1,0:T(8,128)S(1)} %copy.33, f32[4,264,4]{2,1,0:T(8,128)S(1)} %copy.35), kind=kLoop, calls=%fused_computation.3 | loop fusion | flops 6513408 | bytes 13043712 | tf_op jit(solution)/shard_map/concatenate | solution.py:27
  217.3 15.3 %fusion.1 = f32[4,264,1024]{2,1,0:T(8,128)S(1)} fusion(f32[4,264,1028]{2,1,0:T(8,128)} %get-tuple-element.45, f32[4,264,1028]{2,1,0:T(8,128)S(1)} %get-tuple-element.44, f32[1024]{0:T(1024)S(1)} %fusion.80, f32[4,4,1024]{2,1,0:T(4,128)S(1)} %collective-permute-done.5, f32[4,256,1024]{2,1,0:T(8,128)} %copy-done, f32[4,4,1024]{2,1,0:T(4,128)S(1)} %collective-permute-done.4), kind=kLoop, calls=%fused_computation.8 | loop fusion | flops 20545536 | bytes 43257856 | tf_op jit(solution)/shard_map/div | solution.py:95
  232.7 5.7 %fusion.17 = f32[4,256,1024]{2,1,0:T(8,128)} fusion(f32[4,264,1024]{2,1,0:T(8,128)S(1)} %fusion.1, f32[256]{0:T(256)S(1)} %multiply_add_fusion.3), kind=kLoop, calls=%fused_computation.41 | loop fusion | flops 17825792 | bytes 41944064 | tf_op jit(solution)/shard_map/div | solution.py:105
  238.3 19.0 %reshape.249 = f32[4,16,16,64,16]{4,3,2,1,0:T(8,128)} reshape(f32[4,256,1024]{2,1,0:T(8,128)} %fusion.17) | data formatting | bytes 8388608 | tf_op jit(solution)/shard_map/reshape | solution.py:110
  257.3 12.2 %reduce_sum.45 = f32[4,16,64]{2,1,0:T(8,128)S(1)} reduce(f32[4,16,16,64,16]{4,3,2,1,0:T(8,128)} %reshape.249, f32[]{:T(128)} %constant.64.clone.1), dimensions={2,4}, to_apply=%region_0.0 | reduce | flops 1044480 | bytes 4210692 | tf_op jit(solution)/shard_map/reduce_sum | solution.py:110
  269.6 27.9 %all_gather.6 = f32[4,16,512]{1,0,2:T(4,128)S(1)} all-gather(f32[4,16,64]{1,0,2:T(4,128)S(1)} %copy.36), channel_id=1, replica_groups=mesh['row'=16,'col'=8] {'col'}, dimensions={2}, use_global_device_ids=true | all-gather | bytes 147456 | tf_op jit(solution)/shard_map/all_gather | solution.py:121
  297.5 1.8 convolution_divide_fusion
  299.3 27.6 %all_gather.7 = f32[4,256,64]{2,1,0:T(8,128)S(1)} all-gather(f32[4,16,64]{2,1,0:T(8,128)S(1)} %convolution_divide_fusion), channel_id=1, replica_groups=mesh['row'=16,'col'=8] {'row'}, dimensions={1}, use_global_device_ids=true | all-gather | bytes 278528 | tf_op jit(solution)/shard_map/all_gather | solution.py:132
  326.9 0.4 fusion.28
  327.3 1.9 collective-permute-start.8
  329.3 2.4 collective-permute-start.9
  331.7 2.5 collective-permute-done.9
  334.3 1.8 collective-permute-start.10
  336.1 1.6 collective-permute-start.11
  337.7 3.2 collective-permute-done.11
  340.9 0.6 convolution_bitcast_fusion
  341.5 6.0 %convolution_subtract_fusion = f32[4,256,1024]{2,1,0:T(8,128)S(1)} fusion(f32[4,256,1024]{2,1,0:T(8,128)} %fusion.17, f32[4,256,66]{1,2,0:T(8,128)S(1)} %convolution_bitcast_fusion, f32[1024]{0:T(1024)S(1)} %get-tuple-element.71, s32[1024]{0:T(1024)S(1)} %get-tuple-element.74, f32[1024]{0:T(1024)S(1)} %get-tuple-element.72, ...), kind=kOutput, calls=%fused_computation.65 | convolution fusion | flops 831858688 | bytes 8675592 | tf_op jit(solution)/shard_map/spb,qb->spq/dot_general | solution.py:170
  347.5 3.4 collective-permute-start.12
  350.9 1.9 collective-permute-start.13
  352.9 3.1 collective-permute-done.13
  356.2 0.3 copy.38
  356.5 1.3 collective-permute-start.14
  357.8 0.3 copy.40
  358.1 4.0 collective-permute-start.15
  362.3 0.5 collective-permute-done.15
  363.0 13.9 %fusion.112 = (f32[4]{0:T(128)S(1)}, f32[4,256,1024]{2,1,0:T(8,128)}, f32[4]{0:T(128)S(1)}) fusion(f32[256]{0:T(256)S(1)} %and_convert_fusion, f32[4,256,1024]{2,1,0:T(8,128)} %copy-done.1, f32[4,1,1024]{2,1,0:T(1,128)S(1)} %collective-permute-done.12, f32[4,1,1024]{2,1,0:T(1,128)S(1)} %collective-permute-done.13, f32[1024]{0:T(1024)S(1)} %fusion.92, ...), kind=kLoop, calls=%fused_computation.219 | loop fusion | flops 18874360 | bytes 8434784 | tf_op jit(solution)/shard_map/reduce_sum | solution.py:203
  377.0 78.1 %all-reduce = (f32[1,4]{1,0:T(1,128)S(1)}, f32[1,4]{1,0:T(1,128)S(1)}) all-reduce(f32[1,4]{1,0:T(1,128)S(1)} %bitcast.87, f32[1,4]{1,0:T(1,128)S(1)} %bitcast.88), channel_id=1, replica_groups=mesh['row'=16,'col'=8] {'row','col'}, use_global_device_ids=true, to_apply=%region_6.7 | all-reduce | flops 8 | bytes 64 | tf_op jit(solution)/shard_map/psum | solution.py:204
  455.1 0.6 fusion.98
  (58 shorter events, 2.5 us)
Async XLA Ops:
  5.3 27.8 %collective-permute-start = (f32[4,130,1024]{2,0,1:T(4,128)S(1)}, f32[4,130,1024]{2,0,1:T(4,128)}, u32[]{:S(2)}, u32[]{:S(2)}) collective-permute-start(f32[4,130,1024]{2,0,1:T(4,128)S(1)} %copy.42), channel_id=1, source_target_pairs={{0,8},{8,16},{16,24},{24,32},{32,40},{40,48},{48,56},{56,64},{64,7... | collective-permute-start | bytes 6389768 | tf_op jit(solution)/shard_map/ppermute | solution.py:25
  12.5 7.3 %copy-start.5 = (s32[2,4,1,1]{1,3,2,0:T(1,128)S(1)}, s32[2,4,1,1]{1,3,2,0:T(1,128)}, u32[]{:S(2)}) copy-start(s32[2,4,1,1]{1,3,2,0:T(1,128)} %param.6) | copy-start | bytes 100
  12.5 28.1 %collective-permute-start.1 = (f32[4,130,1024]{2,0,1:T(4,128)}, f32[4,130,1024]{2,0,1:T(4,128)}, u32[]{:S(2)}, u32[]{:S(2)}) collective-permute-start(f32[4,130,1024]{2,0,1:T(4,128)} %copy.43), channel_id=1, source_target_pairs={{8,0},{16,8},{24,16},{32,24},{40,32},{48,40},{56,48},{64,56},{72,6... | collective-permute-start | bytes 6389768 | tf_op jit(solution)/shard_map/ppermute | solution.py:26
  46.8 9.3 %copy-start.4 = (s32[2,4,1,1]{1,3,2,0:T(1,128)S(1)}, s32[2,4,1,1]{1,3,2,0:T(1,128)}, u32[]{:S(2)}) copy-start(s32[2,4,1,1]{1,3,2,0:T(1,128)} %param.7) | copy-start | bytes 100
  46.8 50.1 %copy-start.2 = (f32[4,256,1024]{1,0,2:T(4,128)S(1)}, f32[4,256,1024]{1,0,2:T(4,128)}, u32[]{:S(2)}) copy-start(f32[4,256,1024]{1,0,2:T(4,128)} %copy.28) | copy-start | bytes 12582916
  50.3 46.6 %collective-permute-start.2 = (f32[4,516,130]{1,0,2:T(4,128)S(1)}, f32[4,516,130]{1,0,2:T(4,128)S(1)}, u32[]{:S(2)}, u32[]{:S(2)}) collective-permute-start(f32[4,516,130]{1,0,2:T(4,128)S(1)} %get-tuple-element.42), channel_id=1, source_target_pairs={{0,1},{1,2},{2,3},{3,4},{4,5},{5,6},{6,7},{8,9},{9,10},{10,11},{11... | collective-permute-start | bytes 3219848 | tf_op jit(solution)/shard_map/ppermute | solution.py:25
  54.1 42.8 %collective-permute-start.3 = (f32[4,516,130]{1,0,2:T(4,128)S(1)}, f32[4,516,130]{1,0,2:T(4,128)S(1)}, u32[]{:S(2)}, u32[]{:S(2)}) collective-permute-start(f32[4,516,130]{1,0,2:T(4,128)S(1)} %get-tuple-element.43), channel_id=1, source_target_pairs={{1,0},{2,1},{3,2},{4,3},{5,4},{6,5},{7,6},{9,8},{10,9},{11,10},{12... | collective-permute-start | bytes 3219848 | tf_op jit(solution)/shard_map/ppermute | solution.py:26
  163.2 9.2 %copy-start.3 = (f32[4,256,1024]{2,1,0:T(8,128)S(1)}, f32[4,256,1024]{2,1,0:T(8,128)}, u32[]{:S(2)}) copy-start(f32[4,256,1024]{2,1,0:T(8,128)} %param.4) | copy-start | bytes 12582916
  175.9 24.1 %copy-start = (f32[4,256,1024]{2,1,0:T(8,128)}, f32[4,256,1024]{2,1,0:T(8,128)S(1)}, u32[]{:S(2)}) copy-start(f32[4,256,1024]{2,1,0:T(8,128)S(1)} %fusion.25) | copy-start | bytes 12582916
  176.0 19.8 %collective-permute-start.4 = (f32[4,4,1024]{2,1,0:T(4,128)S(1)}, f32[4,4,1024]{2,1,0:T(4,128)S(1)}, u32[]{:S(2)}, u32[]{:S(2)}) collective-permute-start(f32[4,4,1024]{2,1,0:T(4,128)S(1)} %get-tuple-element.53), channel_id=1, source_target_pairs={{0,8},{8,16},{16,24},{24,32},{32,40},{40,48},{48,56},{56,64},{64,7... | collective-permute-start | bytes 196616 | tf_op jit(solution)/shard_map/ppermute | solution.py:25
  193.8 5.6 %collective-permute-start.5 = (f32[4,4,1024]{2,1,0:T(4,128)S(1)}, f32[4,4,1024]{2,1,0:T(4,128)S(1)}, u32[]{:S(2)}, u32[]{:S(2)}) collective-permute-start(f32[4,4,1024]{2,1,0:T(4,128)S(1)} %get-tuple-element.54), channel_id=1, source_target_pairs={{8,0},{16,8},{24,16},{32,24},{40,32},{48,40},{56,48},{64,56},{72,6... | collective-permute-start | bytes 196616 | tf_op jit(solution)/shard_map/ppermute | solution.py:26
  200.4 5.9 %collective-permute-start.6 = (f32[4,264,4]{1,2,0:T(4,128)S(1)}, f32[4,264,4]{1,2,0:T(4,128)S(1)}, u32[]{:S(2)}, u32[]{:S(2)}) collective-permute-start(f32[4,264,4]{1,2,0:T(4,128)S(1)} %copy.32), channel_id=1, source_target_pairs={{0,1},{1,2},{2,3},{3,4},{4,5},{5,6},{6,7},{8,9},{9,10},{10,11},{11... | collective-permute-start | bytes 50696 | tf_op jit(solution)/shard_map/ppermute | solution.py:25
  204.8 4.8 %collective-permute-start.7 = (f32[4,264,4]{1,2,0:T(4,128)S(1)}, f32[4,264,4]{1,2,0:T(4,128)S(1)}, u32[]{:S(2)}, u32[]{:S(2)}) collective-permute-start(f32[4,264,4]{1,2,0:T(4,128)S(1)} %copy.34), channel_id=1, source_target_pairs={{1,0},{2,1},{3,2},{4,3},{5,4},{6,5},{7,6},{9,8},{10,9},{11,10},{12... | collective-permute-start | bytes 50696 | tf_op jit(solution)/shard_map/ppermute | solution.py:26
  327.3 4.4 collective-permute-start.8
  329.3 4.9 %collective-permute-start.9 = (f32[4,1,64]{2,1,0:T(1,128)S(1)}, f32[4,1,64]{2,1,0:T(1,128)S(1)}, u32[]{:S(2)}, u32[]{:S(2)}) collective-permute-start(f32[4,1,64]{2,1,0:T(1,128)S(1)} %get-tuple-element.60), channel_id=1, source_target_pairs={{8,0},{16,8},{24,16},{32,24},{40,32},{48,40},{56,48},{64,56},{72,6... | collective-permute-start | bytes 3080 | tf_op jit(solution)/shard_map/ppermute | solution.py:26
  334.3 3.4 collective-permute-start.10
  336.1 4.8 %collective-permute-start.11 = (f32[4,18,1]{2,1,0:T(8,128)S(1)}, f32[4,18,1]{2,1,0:T(8,128)S(1)}, u32[]{:S(2)}, u32[]{:S(2)}) collective-permute-start(f32[4,18,1]{2,1,0:T(8,128)S(1)} %get-tuple-element.58), channel_id=1, source_target_pairs={{1,0},{2,1},{3,2},{4,3},{5,4},{6,5},{7,6},{9,8},{10,9},{11,10},{12... | collective-permute-start | bytes 872 | tf_op jit(solution)/shard_map/ppermute | solution.py:26
  347.5 8.5 %copy-start.1 = (f32[4,256,1024]{2,1,0:T(8,128)}, f32[4,256,1024]{2,1,0:T(8,128)S(1)}, u32[]{:S(2)}) copy-start(f32[4,256,1024]{2,1,0:T(8,128)S(1)} %convolution_subtract_fusion) | copy-start | bytes 12582916
  347.5 5.3 %collective-permute-start.12 = (f32[4,1,1024]{2,1,0:T(1,128)S(1)}, f32[4,1,1024]{2,1,0:T(1,128)S(1)}, u32[]{:S(2)}, u32[]{:S(2)}) collective-permute-start(f32[4,1,1024]{2,1,0:T(1,128)S(1)} %get-tuple-element.52), channel_id=1, source_target_pairs={{0,8},{8,16},{16,24},{24,32},{32,40},{40,48},{48,56},{56,64},{64,7... | collective-permute-start | bytes 49160 | tf_op jit(solution)/shard_map/ppermute | solution.py:25
  350.9 5.1 %collective-permute-start.13 = (f32[4,1,1024]{2,1,0:T(1,128)S(1)}, f32[4,1,1024]{2,1,0:T(1,128)S(1)}, u32[]{:S(2)}, u32[]{:S(2)}) collective-permute-start(f32[4,1,1024]{2,1,0:T(1,128)S(1)} %get-tuple-element.51), channel_id=1, source_target_pairs={{8,0},{16,8},{24,16},{32,24},{40,32},{48,40},{56,48},{64,56},{72,6... | collective-permute-start | bytes 49160 | tf_op jit(solution)/shard_map/ppermute | solution.py:26
  356.5 5.6 %collective-permute-start.14 = (f32[4,258,1]{1,0,2:T(4,128)S(1)}, f32[4,258,1]{1,0,2:T(4,128)S(1)}, u32[]{:S(2)}, u32[]{:S(2)}) collective-permute-start(f32[4,258,1]{1,0,2:T(4,128)S(1)} %copy.38), channel_id=1, source_target_pairs={{1,0},{2,1},{3,2},{4,3},{5,4},{6,5},{7,6},{9,8},{10,9},{11,10},{12... | collective-permute-start | bytes 12392 | tf_op jit(solution)/shard_map/ppermute | solution.py:26
  358.1 4.8 %collective-permute-start.15 = (f32[4,258,1]{1,0,2:T(4,128)S(1)}, f32[4,258,1]{1,0,2:T(4,128)S(1)}, u32[]{:S(2)}, u32[]{:S(2)}) collective-permute-start(f32[4,258,1]{1,0,2:T(4,128)S(1)} %copy.40), channel_id=1, source_target_pairs={{0,1},{1,2},{2,3},{3,4},{4,5},{5,6},{6,7},{8,9},{9,10},{10,11},{11... | collective-permute-start | bytes 12392 | tf_op jit(solution)/shard_map/ppermute | solution.py:25
where the time goes:
time: 458 us; the launch traced here: 456 us
  blocking collectives  134 us (29%)
  other arithmetic  102 us (22%)
  local copies, waits for them, and re-layouts  83.4 us (18%)
  waiting for transfers between devices  71.2 us (16%)
  starting transfers between devices  55.5 us (12%)
  matrix products  8.74 us (2%)
    psum x1, blocking collectives, body(): height_all, slope_all = lax.psum((height_sq, slope_sum), ('row', 'col'))  78.1 us
    ppermute x8, waiting for transfers between devices, with_halo(): before = lax.ppermute(last, axis, up)  54.4 us
    ppermute x8, starting transfers between devices, with_halo(): before = lax.ppermute(last, axis, up)  41.4 us
    concatenate x4, other arithmetic, with_halo(): value = jnp.concatenate([before, value, after], axis=dim)  37.5 us
    all_gather x1, blocking collectives, long_cols(): portion = lax.all_gather(coarse, 'col', axis=2, tiled=True)  27.9 us
    all_gather x1, blocking collectives, long_rows(): portion = lax.all_gather(surface, 'row', axis=1, tiled=True)  27.6 us
    unnamed x18, local copies, waits for them, and re-layouts  24.7 us
    gather x12, local copies, waits for them, and re-layouts  21.5 us
  transfers between devices with their start and end apart: 16, of which 9 were waited for; matrix products, arithmetic and copies ran while one was open for 4% of the time, Pallas kernels for 0%

commit v1 on v0

--- a/solution.py
+++ b/solution.py
@@ -201,7 +201,9 @@
     slope_field = slopes(band_field)
     height_sq = jnp.sum(band_field * band_field, axis=(1, 2))
     slope_sum = jnp.sum(slope_field, axis=(1, 2))
-    height_all, slope_all = lax.psum((height_sq, slope_sum), ("row", "col"))
+    height_all, slope_all = lax.psum(
+        lax.psum((height_sq, slope_sum), axis_name="col"), axis_name="row"
+    )
     total_cells = height * lax.axis_size("row") * length * lax.axis_size("col")
     surface_params = jnp.sqrt(jnp.stack([height_all, slope_all]) / total_cells + EPSILON)
     return (band_field, slope_field, surface_params)

time: 458 us -> 441 us (0.963)
  the two profiles are of different devices: /device:TPU:1 before, /device:TPU:65 now
where the time goes in v1:
time: 441 us; the launch traced here: 439 us
  blocking collectives  116 us (26%)
  other arithmetic  102 us (23%)
  local copies, waits for them, and re-layouts  83.1 us (19%)
  waiting for transfers between devices  80.5 us (18%)
  starting transfers between devices  46.7 us (11%)
  matrix products  8.74 us (2%)
    ppermute x8, waiting for transfers between devices, with_halo(): before = lax.ppermute(last, axis, up)  64.9 us
    psum x1, blocking collectives, body(): lax.psum(lax.psum((height_sq, slope_sum), axis_name='col'), axis_name='row')  43 us
    concatenate x4, other arithmetic, with_halo(): value = jnp.concatenate([before, value, after], axis=dim)  37.5 us
    ppermute x8, starting transfers between devices, with_halo(): before = lax.ppermute(last, axis, up)  30.9 us
    all_gather x1, blocking collectives, long_rows(): portion = lax.all_gather(surface, 'row', axis=1, tiled=True)  28.7 us
    all_gather x1, blocking collectives, long_cols(): portion = lax.all_gather(coarse, 'col', axis=2, tiled=True)  28 us
    unnamed x18, local copies, waits for them, and re-layouts  24.7 us
    gather x12, local copies, waits for them, and re-layouts  21.3 us
  transfers between devices with their start and end apart: 16, of which 9 were waited for; matrix products, arithmetic and copies ran while one was open for 4% of the time, Pallas kernels for 0%

profile of v1, /device:TPU:65, one launch (start us, length us, event | category | flops | bytes accessed | tf_op | source)
XLA Modules:
  0.0 438.7 jit_solution(10818376097326824625)
XLA Ops:
  0.6 3.2 fusion.118
  3.9 1.4 copy.42
  5.3 3.7 collective-permute-start
  8.9 2.7 copy.43
  11.7 2.0 collective-permute-start.1
  13.7 5.2 %copy.28 = f32[4,256,1024]{1,0,2:T(4,128)} copy(f32[4,256,1024]{2,1,0:T(8,128)} %param.5) | data formatting | bytes 8388608 | tf_op args[1]
  19.1 13.1 %collective-permute-done = f32[4,130,1024]{2,0,1:T(4,128)} collective-permute-done((f32[4,130,1024]{2,0,1:T(4,128)S(1)}, f32[4,130,1024]{2,0,1:T(4,128)}, u32[]{:S(2)}, u32[]{:S(2)}) %collective-permute-start) | collective-permute-done | bytes 2129952 | tf_op jit(solution)/shard_map/ppermute | solution.py:25
  32.3 6.3 %copy.27 = f32[4,130,1024]{1,0,2:T(4,128)} copy(f32[4,130,1024]{2,0,1:T(4,128)} %collective-permute-done) | data formatting | bytes 4259840 | tf_op jit(solution)/shard_map/ppermute | solution.py:25
  38.5 1.3 collective-permute-done.1
  39.8 6.2 %copy.29 = f32[4,130,1024]{1,0,2:T(4,128)} copy(f32[4,130,1024]{2,0,1:T(4,128)} %collective-permute-done.1) | data formatting | bytes 4259840 | tf_op jit(solution)/shard_map/ppermute | solution.py:26
  46.0 3.5 pad_maximum_fusion.13
  49.5 3.3 collective-permute-start.2
  52.8 1.5 collective-permute-start.3
  54.9 51.2 %collective-permute-done.2 = f32[4,516,130]{1,0,2:T(4,128)S(1)} collective-permute-done((f32[4,516,130]{1,0,2:T(4,128)S(1)}, f32[4,516,130]{1,0,2:T(4,128)S(1)}, u32[]{:S(2)}, u32[]{:S(2)}) %collective-permute-start.2) | collective-permute-done | bytes 1073312 | tf_op jit(solution)/shard_map/ppermute | solution.py:25
  106.2 29.5 %pad_maximum_fusion = f32[4,516,1284]{1,0,2:T(4,128)} fusion(f32[4,516,130]{1,0,2:T(4,128)S(1)} %collective-permute-done.3, f32[4,130,1024]{1,0,2:T(4,128)} %copy.29, f32[4,256,1024]{1,0,2:T(4,128)S(1)} %copy-done.2, f32[4,130,1024]{1,0,2:T(4,128)} %copy.27, f32[4,516,130]{1,0,2:T(4,128)S(1)} %collective-permute-done.2), kind=kLoop, calls=%fused_computation.2 | loop fusion | flops 10600704 | bytes 21201408 | tf_op jit(solution)/shard_map/concatenate | solution.py:27
  135.6 15.3 %copy.30 = f32[4,516,1284]{2,1,0:T(8,128)} copy(f32[4,516,1284]{1,0,2:T(4,128)} %pad_maximum_fusion) | data formatting | bytes 21201408
  150.9 21.3 %while.1 = (s32[]{:T(128)}, f32[4,516,1284]{2,1,0:T(8,128)}, s32[4,3]{1,0:T(4,128)S(1)}, f32[4,259,1027]{2,1,0:T(8,128)}, s32[]{:T(128)}) while((s32[]{:T(128)}, f32[4,516,1284]{2,1,0:T(8,128)}, s32[4,3]{1,0:T(4,128)S(1)}, f32[4,259,1027]{2,1,0:T(8,128)}, s32[]{:T(128)}) %tuple.51), condition=%wide.while_cond, body=%wide.while_body.sunk | while | flops 2 | bytes 2435185 | solution.py:68
  150.9 0.6 fusion.124
  151.5 4.8 %dynamic-slice_dynamic-update-slice_fusion.2 = f32[4,259,1027]{2,1,0:T(8,128)} fusion(f32[4,259,1027]{2,1,0:T(8,128)} %get-tuple-element.120, s32[]{:T(128)} %get-tuple-element.117, f32[4,516,1284]{2,1,0:T(8,128)} %get-tuple-element.123, s32[]{:T(128)} %bitcast.84, s32[]{:T(128)} %bitcast.85, s32[]{:T(128)} %bitcast.86), kind=kLoop, calls=%fused_computation.clone.1 | loop fusion | bytes 2435072 | tf_op jit(solution)/shard_map/vmap()/gather
  156.3 0.6 fusion.124
  156.9 4.7 %dynamic-slice_dynamic-update-slice_fusion.2 = f32[4,259,1027]{2,1,0:T(8,128)} fusion(f32[4,259,1027]{2,1,0:T(8,128)} %get-tuple-element.120, s32[]{:T(128)} %get-tuple-element.117, f32[4,516,1284]{2,1,0:T(8,128)} %get-tuple-element.123, s32[]{:T(128)} %bitcast.84, s32[]{:T(128)} %bitcast.85, s32[]{:T(128)} %bitcast.86), kind=kLoop, calls=%fused_computation.clone.1 | loop fusion | bytes 2435072 | tf_op jit(solution)/shard_map/vmap()/gather
  161.6 0.6 fusion.124
  162.2 4.7 %dynamic-slice_dynamic-update-slice_fusion.2 = f32[4,259,1027]{2,1,0:T(8,128)} fusion(f32[4,259,1027]{2,1,0:T(8,128)} %get-tuple-element.120, s32[]{:T(128)} %get-tuple-element.117, f32[4,516,1284]{2,1,0:T(8,128)} %get-tuple-element.123, s32[]{:T(128)} %bitcast.84, s32[]{:T(128)} %bitcast.85, s32[]{:T(128)} %bitcast.86), kind=kLoop, calls=%fused_computation.clone.1 | loop fusion | bytes 2435072 | tf_op jit(solution)/shard_map/vmap()/gather
  166.9 0.6 fusion.124
  167.5 4.7 %dynamic-slice_dynamic-update-slice_fusion.2 = f32[4,259,1027]{2,1,0:T(8,128)} fusion(f32[4,259,1027]{2,1,0:T(8,128)} %get-tuple-element.120, s32[]{:T(128)} %get-tuple-element.117, f32[4,516,1284]{2,1,0:T(8,128)} %get-tuple-element.123, s32[]{:T(128)} %bitcast.84, s32[]{:T(128)} %bitcast.85, s32[]{:T(128)} %bitcast.86), kind=kLoop, calls=%fused_computation.clone.1 | loop fusion | bytes 2435072 | tf_op jit(solution)/shard_map/vmap()/gather
  172.2 9.2 %multiply_add_fusion = f32[4,256,1027]{2,1,0:T(8,128)S(1)} fusion(f32[4,259,1027]{2,1,0:T(8,128)} %get-tuple-element.10, f32[4]{0:T(128)S(1)} %get-tuple-element.69, f32[4]{0:T(128)S(1)} %get-tuple-element.64, f32[4]{0:T(128)S(1)} %get-tuple-element.66, f32[4]{0:T(128)S(1)} %get-tuple-element.65), kind=kLoop, calls=%fused_computation.5 | loop fusion | flops 7361536 | bytes 21033024 | tf_op jit(solution)/shard_map/vmap()/add | solution.py:47
  181.5 3.4 fusion.25
  184.9 7.5 %collective-permute-start.4 = (f32[4,4,1024]{2,1,0:T(4,128)S(1)}, f32[4,4,1024]{2,1,0:T(4,128)S(1)}, u32[]{:S(2)}, u32[]{:S(2)}) collective-permute-start(f32[4,4,1024]{2,1,0:T(4,128)S(1)} %get-tuple-element.55), channel_id=1, source_target_pairs={{0,8},{8,16},{16,24},{24,32},{32,40},{40,48},{48,56},{56,64},{64,7... | collective-permute-start | bytes 196616 | tf_op jit(solution)/shard_map/ppermute | solution.py:25
  192.4 1.9 collective-permute-start.5
  194.4 3.9 collective-permute-done.5
  198.3 0.6 pad_maximum_fusion.2
  199.0 0.3 copy.32
  199.3 4.1 collective-permute-start.6
  203.4 0.3 copy.34
  203.7 1.5 collective-permute-start.7
  205.5 3.3 collective-permute-done.7
  209.1 7.4 %maximum_maximum_fusion = (f32[4,264,1028]{2,1,0:T(8,128)S(1)}, f32[4,264,1028]{2,1,0:T(8,128)}) fusion(f32[4,4,1024]{2,1,0:T(4,128)S(1)} %collective-permute-done.5, f32[4,256,1024]{2,1,0:T(8,128)} %copy-done, f32[4,4,1024]{2,1,0:T(4,128)S(1)} %collective-permute-done.4, f32[4,264,4]{2,1,0:T(8,128)S(1)} %copy.33, f32[4,264,4]{2,1,0:T(8,128)S(1)} %copy.35), kind=kLoop, calls=%fused_computation.3 | loop fusion | flops 6513408 | bytes 13043712 | tf_op jit(solution)/shard_map/concatenate | solution.py:27
  216.5 15.3 %fusion.1 = f32[4,264,1024]{2,1,0:T(8,128)S(1)} fusion(f32[4,264,1028]{2,1,0:T(8,128)} %get-tuple-element.47, f32[4,264,1028]{2,1,0:T(8,128)S(1)} %get-tuple-element.46, f32[1024]{0:T(1024)S(1)} %fusion.80, f32[4,4,1024]{2,1,0:T(4,128)S(1)} %collective-permute-done.5, f32[4,256,1024]{2,1,0:T(8,128)} %copy-done, f32[4,4,1024]{2,1,0:T(4,128)S(1)} %collective-permute-done.4), kind=kLoop, calls=%fused_computation.8 | loop fusion | flops 20545536 | bytes 43257856 | tf_op jit(solution)/shard_map/div | solution.py:95
  231.8 5.7 %fusion.17 = f32[4,256,1024]{2,1,0:T(8,128)} fusion(f32[4,264,1024]{2,1,0:T(8,128)S(1)} %fusion.1, f32[256]{0:T(256)S(1)} %multiply_add_fusion.3), kind=kLoop, calls=%fused_computation.41 | loop fusion | flops 17825792 | bytes 41944064 | tf_op jit(solution)/shard_map/div | solution.py:105
  237.5 19.0 %reshape.249 = f32[4,16,16,64,16]{4,3,2,1,0:T(8,128)} reshape(f32[4,256,1024]{2,1,0:T(8,128)} %fusion.17) | data formatting | bytes 8388608 | tf_op jit(solution)/shard_map/reshape | solution.py:110
  256.5 12.2 %reduce_sum.45 = f32[4,16,64]{2,1,0:T(8,128)S(1)} reduce(f32[4,16,16,64,16]{4,3,2,1,0:T(8,128)} %reshape.249, f32[]{:T(128)} %constant.64.clone.1), dimensions={2,4}, to_apply=%region_0.0 | reduce | flops 1044480 | bytes 4210692 | tf_op jit(solution)/shard_map/reduce_sum | solution.py:110
  268.8 28.0 %all_gather.6 = f32[4,16,512]{1,0,2:T(4,128)S(1)} all-gather(f32[4,16,64]{1,0,2:T(4,128)S(1)} %copy.36), channel_id=1, replica_groups=mesh['row'=16,'col'=8] {'col'}, dimensions={2}, use_global_device_ids=true | all-gather | bytes 147456 | tf_op jit(solution)/shard_map/all_gather | solution.py:121
  296.8 1.8 convolution_divide_fusion
  298.6 28.7 %all_gather.7 = f32[4,256,64]{2,1,0:T(8,128)S(1)} all-gather(f32[4,16,64]{2,1,0:T(8,128)S(1)} %convolution_divide_fusion), channel_id=1, replica_groups=mesh['row'=16,'col'=8] {'row'}, dimensions={1}, use_global_device_ids=true | all-gather | bytes 278528 | tf_op jit(solution)/shard_map/all_gather | solution.py:132
  327.3 0.4 fusion.28
  327.7 3.5 collective-permute-start.8
  331.2 1.9 collective-permute-start.9
  333.2 3.0 collective-permute-done.9
  336.2 1.3 collective-permute-start.10
  337.5 1.6 collective-permute-start.11
  339.1 3.2 collective-permute-done.11
  342.4 0.6 convolution_bitcast_fusion
  342.9 6.0 %convolution_subtract_fusion = f32[4,256,1024]{2,1,0:T(8,128)S(1)} fusion(f32[4,256,1024]{2,1,0:T(8,128)} %fusion.17, f32[4,256,66]{1,2,0:T(8,128)S(1)} %convolution_bitcast_fusion, f32[1024]{0:T(1024)S(1)} %get-tuple-element.73, s32[1024]{0:T(1024)S(1)} %get-tuple-element.76, f32[1024]{0:T(1024)S(1)} %get-tuple-element.74, ...), kind=kOutput, calls=%fused_computation.65 | convolution fusion | flops 831858688 | bytes 8675592 | tf_op jit(solution)/shard_map/spb,qb->spq/dot_general | solution.py:170
  349.0 3.1 collective-permute-start.12
  352.1 4.1 collective-permute-start.13
  356.2 0.9 collective-permute-done.13
  357.4 0.3 copy.38
  357.6 1.3 collective-permute-start.14
  359.2 4.4 collective-permute-start.15
  363.8 0.5 collective-permute-done.15
  364.6 13.9 %fusion.112 = (f32[4]{0:T(128)S(1)}, f32[4,256,1024]{2,1,0:T(8,128)}, f32[4]{0:T(128)S(1)}) fusion(f32[256]{0:T(256)S(1)} %and_convert_fusion, f32[4,256,1024]{2,1,0:T(8,128)} %copy-done.1, f32[4,1,1024]{2,1,0:T(1,128)S(1)} %collective-permute-done.12, f32[4,1,1024]{2,1,0:T(1,128)S(1)} %collective-permute-done.13, f32[1024]{0:T(1024)S(1)} %fusion.92, ...), kind=kLoop, calls=%fused_computation.219 | loop fusion | flops 18874360 | bytes 8434784 | tf_op jit(solution)/shard_map/reduce_sum | solution.py:203
  378.5 16.6 %all-reduce.1 = (f32[4]{0:T(128)S(1)}, f32[4]{0:T(128)S(1)}) all-reduce(f32[4]{0:T(128)S(1)} %get-tuple-element.39, f32[4]{0:T(128)S(1)} %get-tuple-element.52), channel_id=1, replica_groups=mesh['row'=16,'col'=8] {'col'}, use_global_device_ids=true, to_apply=%region_7.8 | all-reduce | flops 8 | bytes 64 | tf_op jit(solution)/shard_map/psum | solution.py:205
  395.1 43.0 %all-reduce = (f32[1,4]{1,0:T(1,128)S(1)}, f32[1,4]{1,0:T(1,128)S(1)}) all-reduce(f32[1,4]{1,0:T(1,128)S(1)} %bitcast.87, f32[1,4]{1,0:T(1,128)S(1)} %bitcast.88), channel_id=1, replica_groups=mesh['row'=16,'col'=8] {'row'}, use_global_device_ids=true, to_apply=%region_8.9 | all-reduce | flops 8 | bytes 64 | tf_op jit(solution)/shard_map/psum | solution.py:204
  438.1 0.6 fusion.98
  (59 shorter events, 2.8 us)
Async XLA Ops:
  5.3 27.0 %collective-permute-start = (f32[4,130,1024]{2,0,1:T(4,128)S(1)}, f32[4,130,1024]{2,0,1:T(4,128)}, u32[]{:S(2)}, u32[]{:S(2)}) collective-permute-start(f32[4,130,1024]{2,0,1:T(4,128)S(1)} %copy.42), channel_id=1, source_target_pairs={{0,8},{8,16},{16,24},{24,32},{32,40},{40,48},{48,56},{56,64},{64,7... | collective-permute-start | bytes 6389768 | tf_op jit(solution)/shard_map/ppermute | solution.py:25
  11.7 7.3 %copy-start.5 = (s32[2,4,1,1]{1,3,2,0:T(1,128)S(1)}, s32[2,4,1,1]{1,3,2,0:T(1,128)}, u32[]{:S(2)}) copy-start(s32[2,4,1,1]{1,3,2,0:T(1,128)} %param.6) | copy-start | bytes 100
  11.7 28.1 %collective-permute-start.1 = (f32[4,130,1024]{2,0,1:T(4,128)}, f32[4,130,1024]{2,0,1:T(4,128)}, u32[]{:S(2)}, u32[]{:S(2)}) collective-permute-start(f32[4,130,1024]{2,0,1:T(4,128)} %copy.43), channel_id=1, source_target_pairs={{8,0},{16,8},{24,16},{32,24},{40,32},{48,40},{56,48},{64,56},{72,6... | collective-permute-start | bytes 6389768 | tf_op jit(solution)/shard_map/ppermute | solution.py:26
  46.0 8.8 %copy-start.4 = (s32[2,4,1,1]{1,3,2,0:T(1,128)S(1)}, s32[2,4,1,1]{1,3,2,0:T(1,128)}, u32[]{:S(2)}) copy-start(s32[2,4,1,1]{1,3,2,0:T(1,128)} %param.7) | copy-start | bytes 100
  46.0 60.2 %copy-start.2 = (f32[4,256,1024]{1,0,2:T(4,128)S(1)}, f32[4,256,1024]{1,0,2:T(4,128)}, u32[]{:S(2)}) copy-start(f32[4,256,1024]{1,0,2:T(4,128)} %copy.28) | copy-start | bytes 12582916
  49.5 56.7 %collective-permute-start.2 = (f32[4,516,130]{1,0,2:T(4,128)S(1)}, f32[4,516,130]{1,0,2:T(4,128)S(1)}, u32[]{:S(2)}, u32[]{:S(2)}) collective-permute-start(f32[4,516,130]{1,0,2:T(4,128)S(1)} %get-tuple-element.44), channel_id=1, source_target_pairs={{0,1},{1,2},{2,3},{3,4},{4,5},{5,6},{6,7},{8,9},{9,10},{10,11},{11... | collective-permute-start | bytes 3219848 | tf_op jit(solution)/shard_map/ppermute | solution.py:25
  52.8 53.3 %collective-permute-start.3 = (f32[4,516,130]{1,0,2:T(4,128)S(1)}, f32[4,516,130]{1,0,2:T(4,128)S(1)}, u32[]{:S(2)}, u32[]{:S(2)}) collective-permute-start(f32[4,516,130]{1,0,2:T(4,128)S(1)} %get-tuple-element.45), channel_id=1, source_target_pairs={{1,0},{2,1},{3,2},{4,3},{5,4},{6,5},{7,6},{9,8},{10,9},{11,10},{12... | collective-permute-start | bytes 3219848 | tf_op jit(solution)/shard_map/ppermute | solution.py:26
  172.2 9.2 %copy-start.3 = (f32[4,256,1024]{2,1,0:T(8,128)S(1)}, f32[4,256,1024]{2,1,0:T(8,128)}, u32[]{:S(2)}) copy-start(f32[4,256,1024]{2,1,0:T(8,128)} %param.4) | copy-start | bytes 12582916
  184.9 13.9 %copy-start = (f32[4,256,1024]{2,1,0:T(8,128)}, f32[4,256,1024]{2,1,0:T(8,128)S(1)}, u32[]{:S(2)}) copy-start(f32[4,256,1024]{2,1,0:T(8,128)S(1)} %fusion.25) | copy-start | bytes 12582916
  184.9 9.4 %collective-permute-start.4 = (f32[4,4,1024]{2,1,0:T(4,128)S(1)}, f32[4,4,1024]{2,1,0:T(4,128)S(1)}, u32[]{:S(2)}, u32[]{:S(2)}) collective-permute-start(f32[4,4,1024]{2,1,0:T(4,128)S(1)} %get-tuple-element.55), channel_id=1, source_target_pairs={{0,8},{8,16},{16,24},{24,32},{32,40},{40,48},{48,56},{56,64},{64,7... | collective-permute-start | bytes 196616 | tf_op jit(solution)/shard_map/ppermute | solution.py:25
  192.4 5.8 %collective-permute-start.5 = (f32[4,4,1024]{2,1,0:T(4,128)S(1)}, f32[4,4,1024]{2,1,0:T(4,128)S(1)}, u32[]{:S(2)}, u32[]{:S(2)}) collective-permute-start(f32[4,4,1024]{2,1,0:T(4,128)S(1)} %get-tuple-element.56), channel_id=1, source_target_pairs={{8,0},{16,8},{24,16},{32,24},{40,32},{48,40},{56,48},{64,56},{72,6... | collective-permute-start | bytes 196616 | tf_op jit(solution)/shard_map/ppermute | solution.py:26
  199.3 5.9 %collective-permute-start.6 = (f32[4,264,4]{1,2,0:T(4,128)S(1)}, f32[4,264,4]{1,2,0:T(4,128)S(1)}, u32[]{:S(2)}, u32[]{:S(2)}) collective-permute-start(f32[4,264,4]{1,2,0:T(4,128)S(1)} %copy.32), channel_id=1, source_target_pairs={{0,1},{1,2},{2,3},{3,4},{4,5},{5,6},{6,7},{8,9},{9,10},{10,11},{11... | collective-permute-start | bytes 50696 | tf_op jit(solution)/shard_map/ppermute | solution.py:25
  203.7 5.1 %collective-permute-start.7 = (f32[4,264,4]{1,2,0:T(4,128)S(1)}, f32[4,264,4]{1,2,0:T(4,128)S(1)}, u32[]{:S(2)}, u32[]{:S(2)}) collective-permute-start(f32[4,264,4]{1,2,0:T(4,128)S(1)} %copy.34), channel_id=1, source_target_pairs={{1,0},{2,1},{3,2},{4,3},{5,4},{6,5},{7,6},{9,8},{10,9},{11,10},{12... | collective-permute-start | bytes 50696 | tf_op jit(solution)/shard_map/ppermute | solution.py:26
  327.7 5.5 %collective-permute-start.8 = (f32[4,1,64]{2,1,0:T(1,128)S(1)}, f32[4,1,64]{2,1,0:T(1,128)S(1)}, u32[]{:S(2)}, u32[]{:S(2)}) collective-permute-start(f32[4,1,64]{2,1,0:T(1,128)S(1)} %get-tuple-element.61), channel_id=1, source_target_pairs={{0,8},{8,16},{16,24},{24,32},{32,40},{40,48},{48,56},{56,64},{64,7... | collective-permute-start | bytes 3080 | tf_op jit(solution)/shard_map/ppermute | solution.py:25
  331.2 4.9 %collective-permute-start.9 = (f32[4,1,64]{2,1,0:T(1,128)S(1)}, f32[4,1,64]{2,1,0:T(1,128)S(1)}, u32[]{:S(2)}, u32[]{:S(2)}) collective-permute-start(f32[4,1,64]{2,1,0:T(1,128)S(1)} %get-tuple-element.62), channel_id=1, source_target_pairs={{8,0},{16,8},{24,16},{32,24},{40,32},{48,40},{56,48},{64,56},{72,6... | collective-permute-start | bytes 3080 | tf_op jit(solution)/shard_map/ppermute | solution.py:26
  336.2 2.9 collective-permute-start.10
  337.5 4.8 %collective-permute-start.11 = (f32[4,18,1]{2,1,0:T(8,128)S(1)}, f32[4,18,1]{2,1,0:T(8,128)S(1)}, u32[]{:S(2)}, u32[]{:S(2)}) collective-permute-start(f32[4,18,1]{2,1,0:T(8,128)S(1)} %get-tuple-element.60), channel_id=1, source_target_pairs={{1,0},{2,1},{3,2},{4,3},{5,4},{6,5},{7,6},{9,8},{10,9},{11,10},{12... | collective-permute-start | bytes 872 | tf_op jit(solution)/shard_map/ppermute | solution.py:26
  348.9 8.2 %copy-start.1 = (f32[4,256,1024]{2,1,0:T(8,128)}, f32[4,256,1024]{2,1,0:T(8,128)S(1)}, u32[]{:S(2)}) copy-start(f32[4,256,1024]{2,1,0:T(8,128)S(1)} %convolution_subtract_fusion) | copy-start | bytes 12582916
  349.0 7.2 %collective-permute-start.12 = (f32[4,1,1024]{2,1,0:T(1,128)S(1)}, f32[4,1,1024]{2,1,0:T(1,128)S(1)}, u32[]{:S(2)}, u32[]{:S(2)}) collective-permute-start(f32[4,1,1024]{2,1,0:T(1,128)S(1)} %get-tuple-element.54), channel_id=1, source_target_pairs={{0,8},{8,16},{16,24},{24,32},{32,40},{40,48},{48,56},{56,64},{64,7... | collective-permute-start | bytes 49160 | tf_op jit(solution)/shard_map/ppermute | solution.py:25
  352.1 5.1 %collective-permute-start.13 = (f32[4,1,1024]{2,1,0:T(1,128)S(1)}, f32[4,1,1024]{2,1,0:T(1,128)S(1)}, u32[]{:S(2)}, u32[]{:S(2)}) collective-permute-start(f32[4,1,1024]{2,1,0:T(1,128)S(1)} %get-tuple-element.53), channel_id=1, source_target_pairs={{8,0},{16,8},{24,16},{32,24},{40,32},{48,40},{56,48},{64,56},{72,6... | collective-permute-start | bytes 49160 | tf_op jit(solution)/shard_map/ppermute | solution.py:26
  357.6 5.9 %collective-permute-start.14 = (f32[4,258,1]{1,0,2:T(4,128)S(1)}, f32[4,258,1]{1,0,2:T(4,128)S(1)}, u32[]{:S(2)}, u32[]{:S(2)}) collective-permute-start(f32[4,258,1]{1,0,2:T(4,128)S(1)} %copy.38), channel_id=1, source_target_pairs={{1,0},{2,1},{3,2},{4,3},{5,4},{6,5},{7,6},{9,8},{10,9},{11,10},{12... | collective-permute-start | bytes 12392 | tf_op jit(solution)/shard_map/ppermute | solution.py:26
  359.2 5.1 %collective-permute-start.15 = (f32[4,258,1]{1,0,2:T(4,128)S(1)}, f32[4,258,1]{1,0,2:T(4,128)S(1)}, u32[]{:S(2)}, u32[]{:S(2)}) collective-permute-start(f32[4,258,1]{1,0,2:T(4,128)S(1)} %copy.40), channel_id=1, source_target_pairs={{0,1},{1,2},{2,3},{3,4},{4,5},{5,6},{6,7},{8,9},{9,10},{10,11},{11... | collective-permute-start | bytes 12392 | tf_op jit(solution)/shard_map/ppermute | solution.py:25
